TPU v7x, 256 devices: a whole 4x4x8 slice. The times are simulated.
256 devices in a mesh: blk: 8 (over y, x_hi), ctx: 32 (over z, x_lo, core).
Axes of the slice: x: 4 (x_hi: 2, x_lo: 2; x = x_hi * 2 + x_lo), y: 4, z: 8, core: 2. Of those that a mesh axis runs over, the one named last changes fastest.
Arguments:
- tokens: bfloat16 [8, 4096, 1024], P('blk', 'ctx'), may hold values from -16 to 16
- segment_ids: int32 [8, 4096], P('blk', 'ctx'), may hold values from 0 to 3, never falling along the last dimension, each value on 1 to 3072 neighbouring positions
- norm_gain: bfloat16 [8, 2, 1024], P('blk'), may hold values from 0.25 to 1.75
- w_mamba_in: bfloat16 [8, 1024, 2048], P('blk', None, 'ctx'), may hold values from -0.1875 to 0.1875
- w_ssm_param: bfloat16 [8, 1024, 160], P('blk'), may hold values from -0.1875 to 0.1875
- ssm_rate: bfloat16 [8, 32], P('blk'), may hold values from 7.2956085e-05 to 0.059814453
- dt_bias: bfloat16 [8, 32], P('blk'), may hold values from -1 to 1
- skip_gain: bfloat16 [8, 32], P('blk'), may hold values from 0.5 to 1.5
- ssm_norm_gain: bfloat16 [8, 2048], P('blk'), may hold values from 0.25 to 1.75
- w_mamba_out: bfloat16 [8, 2048, 1024], P('blk', 'ctx'), may hold values from -0.125 to 0.125
- w_qkv: bfloat16 [8, 1024, 2048], P('blk', None, 'ctx'), may hold values from -1.5 to 1.5
- w_attn_out: bfloat16 [8, 1024, 1024], P('blk', 'ctx'), may hold values from -0.75 to 0.75
Outputs:
- layer_out: bfloat16 [8, 4096, 1024], P('blk', 'ctx')
Inputs may be any that keep to these rules, and one draw needn't show every extreme that they name: `segment_ids`: within each micro-batch the ids never fall along the sequence; each document holds 1 to 3072 tokens, and one holds exactly that many.
All inputs are finite; a program needn't handle non-finite values.
Results may differ from a plain program's by a relative error of at most 0.015.
Values may be sent and summed in bfloat16 or wider, within the bound.
No kernel may reach another device: no remote copies, remote signals or barrier semaphores. Data moves between devices by JAX's collectives and lax.ppermute only.
A program may use at most 128 MiB of HBM per device.

v0:
```python
import math
import jax
import jax.numpy as jnp
from jax import lax
from jax.sharding import Mesh
from jax.sharding import PartitionSpec as P

INNER = 2048
HEAD_DIM = 64
STATE = 64
QUERY_HEADS = 8
KV_HEADS = 4
ATTN_DIM = 128
SPAN = 64
CTX = ("ctx_0", "ctx_1", "ctx_2")
epsilon = 1e-05
highest = lax.Precision.HIGHEST


def filled_with(value, identity):
    return jax.tree.map(
        lambda part, zero: jnp.zeros_like(part) + jnp.asarray(zero, part.dtype), value, identity
    )


def gathered_once(value, axis):
    leaves = jax.tree.leaves(value)
    turns = sorted(range(len(leaves)), key=lambda k: -leaves[k].size)
    width = (1, *leaves[turns[0]].shape)[-1]
    lines = [
        jnp.pad(leaves[k].reshape(-1), (0, -leaves[k].size % width)).reshape(-1, width)
        for k in turns
    ]
    both, at, found = (lax.all_gather(jnp.concatenate(lines), axis), 0, {})
    for k, line in zip(turns, lines):
        slab = both[:, at : at + len(line)].reshape(len(both), -1)
        found[k] = slab[:, : leaves[k].size].reshape(-1, *leaves[k].shape)
        at += len(line)
    numbers = iter(range(len(leaves)))
    return jax.tree.map(lambda _: found[next(numbers)], value)


def collected_alike(value, axis):
    leaves, found = (jax.tree.leaves(value), {})
    for initial, a in enumerate(leaves):
        if initial not in found:
            alike = [k for k, b in enumerate(leaves) if b.dtype == a.dtype]
            got = (
                gathered_once([leaves[k] for k in alike], axis)
                if len(alike) > 1
                else [lax.all_gather(a, axis)]
            )
            for k, b in zip(alike, got):
                found[k] = b
    numbers = iter(range(len(leaves)))
    return jax.tree.map(lambda _: found[next(numbers)], value)


def entering_2(value, axes, combine, identity):
    before = start = filled_with(value, identity)
    so_far = value
    for axis in reversed(axes):
        size, mine = (lax.axis_size(axis), lax.axis_index(axis))
        pieces = collected_alike(so_far, axis)
        inside, so_far = (start, start)
        for k in range(size):
            passed = k < mine
            so_far = combine(so_far, jax.tree.map(lambda part: part[k], pieces))
            inside = jax.tree.map(lambda new, old: jnp.where(passed, new, old), so_far, inside)
        before = combine(inside, before)
    return before


def joined_along(blocks, dim):
    dims = list(blocks.shape[1:])
    dims[dim] *= blocks.shape[0]
    return jnp.moveaxis(blocks, 0, dim).reshape(dims)


def all_blocks(value, axes, turns):
    blocks = value
    for k in turns:
        blocks = lax.all_gather(blocks, axes[k])
    done = turns[::-1]
    back = [done.index(k) for k in range(len(axes))]
    blocks = blocks.transpose(*back, *range(len(axes), blocks.ndim))
    return blocks.reshape(-1, *value.shape)


def whole_of(value, axes, turns, dim):
    return joined_along(all_blocks(value, axes, turns), dim)


def in_one_piece(arrays, axis, dim, along):
    ends, at = ([], 0)
    for a in arrays[:-1]:
        at += a.shape[along]
        ends.append(at)
    both = jnp.concatenate(arrays, axis=along)
    return tuple(jnp.split(lax.all_gather(both, axis, axis=dim, tiled=True), ends, axis=along))


def from_behind(value, axis, steps):
    count = lax.axis_size(axis)
    pairs = [(source, (source + steps) % count) for source in range(count)]
    return lax.ppermute(value, axis, pairs)


def rms_norm(values, gain):
    values = values.astype(jnp.float32)
    scale = lax.rsqrt(jnp.mean(values * values, axis=-1, keepdims=True) + epsilon)
    return values * scale * gain.astype(jnp.float32)


def span_update(carry, block):
    state, prev_segment = carry
    inner_value, bin_value, cout_value, delta, log_decay, segment = block
    cumul = jnp.cumsum(log_decay, axis=0)
    order = jnp.arange(segment.shape[0])
    allowed = (order[:, None] >= order[None, :]) & (segment[:, None] == segment[None, :])
    differ = cumul[:, None, :] - cumul[None, :, :]
    factor = jnp.where(allowed[:, :, None], jnp.exp(jnp.minimum(differ, 0.0)), 0.0)
    intersection = jnp.dot(cout_value, bin_value.T, precision=highest)
    mixing = factor * intersection[:, :, None] * delta[None, :, :]
    within = jnp.einsum("tsh,shp->thp", mixing, inner_value, precision=highest)
    carried = jnp.where((segment == prev_segment)[:, None], jnp.exp(cumul), 0.0)
    across = jnp.einsum("tn,hpn->thp", cout_value, state, precision=highest) * carried[:, :, None]
    last_segment = segment[-1]
    keeping = (
        jnp.where((segment == last_segment)[:, None], jnp.exp(cumul[-1][None, :] - cumul), 0.0)
        * delta
    )
    fresh = jnp.einsum("sh,shp,sn->hpn", keeping, inner_value, bin_value, precision=highest)
    passing = jnp.where(prev_segment == last_segment, jnp.exp(cumul[-1]), 0.0)
    state = passing[:, None, None] * state + fresh
    return ((state, last_segment), within + across)


def combine_states(earlier, later):
    early_first, early_last, early_pass, early_state = earlier
    late_first, late_last, late_pass, late_state = later
    joined = (late_first == early_last) | (early_last < 0) | (late_first < 0)
    factor = jnp.where(joined, late_pass, 0.0)
    first = jnp.where(early_first < 0, late_first, early_first)
    last = jnp.where(late_last < 0, early_last, late_last)
    return (first, last, early_pass * factor, factor[:, None, None] * early_state + late_state)


def layer_pair(tokens, segment, weights):
    (
        norm_gain,
        w_mamba_in,
        w_ssm_param,
        ssm_rate,
        dt_bias,
        skip_gain,
        ssm_norm_gain,
        w_mamba_out,
        w_qkv,
        w_attn_out,
    ) = weights
    rows = tokens.shape[0]
    heads = ssm_rate.shape[0]
    offset = lax.axis_index(CTX) * rows
    normed = rms_norm(tokens, norm_gain[0]).astype(jnp.bfloat16)
    inner = jnp.dot(
        normed,
        lax.all_gather(w_mamba_in, CTX, axis=1, tiled=True),
        preferred_element_type=jnp.float32,
    ).astype(jnp.bfloat16)
    params = jnp.dot(normed, w_ssm_param, preferred_element_type=jnp.float32)
    bin_value = params[:, :STATE]
    cout_value = params[:, STATE : 2 * STATE]
    delta = jax.nn.softplus(params[:, 2 * STATE :] + dt_bias.astype(jnp.float32))
    log_decay = -delta * ssm_rate.astype(jnp.float32)
    inner_value = inner.astype(jnp.float32).reshape(rows, heads, HEAD_DIM)
    blocks = tuple(
        (
            item.reshape((rows // SPAN, SPAN) + item.shape[1:])
            for item in (inner_value, bin_value, cout_value, delta, log_decay, segment)
        )
    )
    start_carry = (jnp.zeros((heads, HEAD_DIM, STATE), jnp.float32), segment[0])
    (local_state, ignored), mixed = lax.scan(span_update, start_carry, blocks)
    device_decay = jnp.cumsum(log_decay, axis=0)
    through = jnp.where(segment[0] == segment[-1], jnp.exp(device_decay[-1]), 0.0)
    element = (segment[0], segment[-1], through, local_state)
    identity = (
        jnp.array(-1, jnp.int32),
        jnp.array(-1, jnp.int32),
        jnp.ones_like(through),
        jnp.zeros_like(local_state),
    )
    scanned = entering_2(element, CTX, combine_states, identity)
    incoming_segment = scanned[1]
    incoming_state = scanned[3]
    linked = jnp.where((segment == incoming_segment)[:, None], jnp.exp(device_decay), 0.0)
    entering = (
        jnp.einsum("tn,hpn->thp", cout_value, incoming_state, precision=highest)
        * linked[:, :, None]
    )
    mixed = (
        mixed.reshape(rows, heads, HEAD_DIM)
        + entering
        + skip_gain.astype(jnp.float32)[None, :, None] * inner_value
    )
    ssm_out = rms_norm(mixed.reshape(rows, INNER), ssm_norm_gain).astype(jnp.bfloat16)
    columns = ssm_out
    first = tokens.astype(jnp.float32) + jnp.dot(
        columns, whole_of(w_mamba_out, CTX, (1, 0, 2), 0), preferred_element_type=jnp.float32
    )
    hidden = rms_norm(first, norm_gain[1]).astype(jnp.bfloat16)
    projected = jnp.dot(
        hidden, lax.all_gather(w_qkv, CTX, axis=1, tiled=True), preferred_element_type=jnp.float32
    ).astype(jnp.bfloat16)
    groups = QUERY_HEADS // KV_HEADS
    query = projected[:, : QUERY_HEADS * ATTN_DIM].reshape(rows, KV_HEADS, groups, ATTN_DIM)
    keys = projected[:, QUERY_HEADS * ATTN_DIM : (QUERY_HEADS + KV_HEADS) * ATTN_DIM]
    values = projected[:, (QUERY_HEADS + KV_HEADS) * ATTN_DIM :]
    positions = offset + jnp.arange(rows)
    scale = 1.0 / math.sqrt(ATTN_DIM)
    top = jnp.full((KV_HEADS, groups, rows), -1e30, jnp.float32)
    key_piece, value_piece, segment_piece = (
        *in_one_piece((keys, values), CTX, 0, 1),
        lax.all_gather(segment, CTX, axis=0, tiled=True),
    )
    count = key_piece.shape[0]
    key_position = jnp.arange(count)
    scores = (
        jnp.einsum(
            "tkgd,skd->kgts",
            query,
            key_piece.reshape(count, KV_HEADS, ATTN_DIM),
            preferred_element_type=jnp.float32,
        )
        * scale
    )
    allowed = (key_position[None, :] <= positions[:, None]) & (
        segment_piece[None, :] == segment[:, None]
    )
    scores = jnp.where(allowed, scores, -1e30)
    new_top = jnp.maximum(top, jnp.max(scores, axis=-1))
    probs = jnp.where(allowed, jnp.exp(scores - new_top[..., None]), 0.0)
    total = jnp.sum(probs, axis=-1)
    attend_context = jnp.einsum(
        "kgts,skd->kgtd",
        probs.astype(jnp.bfloat16),
        value_piece.reshape(count, KV_HEADS, ATTN_DIM),
        preferred_element_type=jnp.float32,
    )
    top, total, context = (new_top, total, attend_context)
    context = context / total[..., None]
    context = (
        jnp.transpose(context, (2, 0, 1, 3))
        .reshape(rows, QUERY_HEADS * ATTN_DIM)
        .astype(jnp.bfloat16)
    )
    columns = context
    result = first + jnp.dot(
        columns,
        lax.all_gather(w_attn_out, CTX, axis=0, tiled=True),
        preferred_element_type=jnp.float32,
    )
    return result.astype(jnp.bfloat16)


def on_device(
    tokens,
    segment_ids,
    norm_gain,
    w_mamba_in,
    w_ssm_param,
    ssm_rate,
    dt_bias,
    skip_gain,
    ssm_norm_gain,
    w_mamba_out,
    w_qkv,
    w_attn_out,
):
    arrived = from_behind(
        (
            norm_gain,
            w_mamba_in,
            w_ssm_param,
            ssm_rate,
            dt_bias,
            skip_gain,
            ssm_norm_gain,
            w_mamba_out,
            w_qkv,
            w_attn_out,
        ),
        "blk",
        1,
    )
    section = tuple((item[0] for item in arrived))
    result = layer_pair(tokens[0], segment_ids[0], section)
    return result[None]


def solution(mesh):
    finer = Mesh(
        mesh.devices.reshape(mesh.shape["blk"], 8, 2, 2), ("blk", "ctx_0", "ctx_1", "ctx_2")
    )
    in_specs = (
        P("blk", CTX, None),
        P("blk", CTX),
        P("blk", None, None),
        P("blk", None, CTX),
        P("blk", None, None),
        P("blk", None),
        P("blk", None),
        P("blk", None),
        P("blk", None),
        P("blk", CTX, None),
        P("blk", None, CTX),
        P("blk", CTX, None),
    )
    out_specs = P("blk", CTX, None)
    return jax.shard_map(
        on_device, mesh=finer, in_specs=in_specs, out_specs=out_specs, check_vma=False
    )
```

profile of v0, /device:TPU:1, one launch (start us, length us, event | category | flops | bytes accessed | tf_op | source)
XLA Modules:
  0.0 555.6 jit_solution(135234453946944221)
XLA Ops:
  6.5 3.6 collective-permute-start.4
  10.1 5.0 collective-permute-done.4
  34.9 50.0 %all-gather.27.cloned.1.call-done = bf16[1,1024,2048]{1,2,0:T(8,128)(2,1)} async-done(((bf16[1,1024,64]{1,2,0:T(8,128)(2,1)}), bf16[1,1024,2048]{1,2,0:T(8,128)(2,1)}) %all-gather.27.cloned.1.call-update) | async-done | bytes 4194320 | tf_op jit(solution)/shard_map/all_gather | solution.py:168
  84.8 3.8 fusion.48
  90.8 76.6 %while.15 = (s32[]{:T(128)}, f32[32,64,64]{2,1,0:T(8,128)S(1)}, s32[]{:T(128)}, f32[2,64,32,64]{1,0,3,2:T(2,128)}, s32[2,64]{1,0:T(2,128)}, /*index=5*/f32[2,64,...) while((s32[]{:T(128)}, f32[32,64,64]{2,1,0:T(8,128)S(1)}, ...), condition=%wide.region_3.4_spmd.clone, body=%wide.region_1.3_spmd.clone.sunk | while | flops 306858144 | bytes 9277010 | solution.py:184
  95.4 3.0 convolution_bitcast_fusion.2
  103.0 25.4 %dynamic_update_slice.6 = f32[2,64,32,64]{1,0,3,2:T(2,128)} dynamic-update-slice(f32[2,64,32,64]{1,0,3,2:T(2,128)} %get-tuple-element.314, f32[1,64,32,64]{1,0,3,2:T(1,128)S(1)} %bitcast.295, s32[]{:T(128)S(6)} %copy.185, s32[]{:T(128)} %constant.29.clone.1..sunk, s32[]{:T(128)} %constant.29.clone.1..sunk, s32[]{:T(128)} %constant.29.clone.1..sunk) | dynamic-update-slice | bytes 1048580 | tf_op jit(solution)/shard_map/while/body/jit(dynamic_update_index_in_dim)/dynamic_update_slice | solution.py:184
  133.6 3.0 convolution_bitcast_fusion.2
  141.3 25.4 %dynamic_update_slice.6 = f32[2,64,32,64]{1,0,3,2:T(2,128)} dynamic-update-slice(f32[2,64,32,64]{1,0,3,2:T(2,128)} %get-tuple-element.314, f32[1,64,32,64]{1,0,3,2:T(1,128)S(1)} %bitcast.295, s32[]{:T(128)S(6)} %copy.185, s32[]{:T(128)} %constant.29.clone.1..sunk, s32[]{:T(128)} %constant.29.clone.1..sunk, s32[]{:T(128)} %constant.29.clone.1..sunk) | dynamic-update-slice | bytes 1048580 | tf_op jit(solution)/shard_map/while/body/jit(dynamic_update_index_in_dim)/dynamic_update_slice | solution.py:184
  172.1 6.0 %collective-permute-done.7 = bf16[1,64,1024]{2,1,0:T(8,128)(2,1)S(1)} collective-permute-done((bf16[1,64,1024]{2,1,0:T(8,128)(2,1)}, bf16[1,64,1024]{2,1,0:T(8,128)(2,1)S(1)}, u32[]{:S(2)}, u32[]{:S(2)}) %collective-permute-start.7) | collective-permute-done | bytes 131104 | tf_op jit(solution)/shard_map/ppermute | solution.py:106
  178.1 4.6 all_gather.79
  186.3 3.8 all-reduce.3
  197.2 26.3 %all-gather.29.cloned.1.call-done = bf16[16,64,1024]{2,1,0:T(8,128)(2,1)} async-done(((bf16[2,64,1024]{2,1,0:T(8,128)(2,1)}), bf16[16,64,1024]{2,1,0:T(8,128)(2,1)}) %all-gather.29.cloned.1.call-update) | async-done | bytes 2097168 | tf_op jit(solution)/shard_map/all_gather | solution.py:83
  228.3 3.1 all-reduce.4
  239.5 8.9 %all-reduce.5 = s32[16]{0:T(128)S(1)} all-reduce(s32[16]{0:T(128)S(1)} %fusion.174), channel_id=5, replica_groups=mesh['blk'=8,'ctx_0'=8,'ctx_1'=2,'ctx_2'=2] {'ctx_0'}, use_global_device_ids=true, to_apply=%add.5 | all-reduce | flops 16 | bytes 128
  267.0 4.7 collective-permute-done.8
  284.3 4.9 copy.121
  289.6 3.3 reshape.485
  299.7 37.0 %all-gather.41.cloned.1.call-done = f32[8,2049,64]{1,2,0:T(8,128)} async-done(((f32[1,2049,64]{1,2,0:T(8,128)}), f32[8,2049,64]{1,2,0:T(8,128)}) %all-gather.41.cloned.1.call-update) | async-done | bytes 4196368 | tf_op jit(solution)/shard_map/all_gather | solution.py:34
  336.7 3.7 fusion.183
  356.5 6.6 %multiply_reduce_fusion = (f32[128]{0:T(128)S(1)}, f32[128,32,64]{0,2,1:T(8,128)S(1)}) fusion(f32[32]{0:T(128)S(1)} %bitcast_convert_fusion, f32[128,2048]{0,1:T(8,128)S(1)} %copy.120, f32[128,32,64]{0,2,1:T(8,128)S(1)} %copy-done.5, f32[128,32]{0,1:T(8,128)S(1)} %exponential_select_fusion.2, f32[32,64,64]{2,1,0:T(8,128)} %bitcast.297, ...), kind=kOutput, calls=%fused_computation.76 | convolution fusion | flops 207748992 | bytes 15780236 | tf_op jit(solution)/shard_map/tn,hpn->thp/dot_general | solution.py:199
  364.5 39.8 %all-gather.33.cloned.1.call-done = bf16[1,1024,2048]{1,2,0:T(8,128)(2,1)} async-done(((bf16[1,1024,64]{1,2,0:T(8,128)(2,1)}), bf16[1,1024,2048]{1,2,0:T(8,128)(2,1)}) %all-gather.33.cloned.1.call-update) | async-done | bytes 4194320 | tf_op jit(solution)/shard_map/all_gather | solution.py:214
  404.2 3.7 fusion.51
  411.3 32.5 %all-gather.9 = s32[1,4096]{1,0:T(1,128)S(1)} all-gather(s32[1,128]{1,0:T(1,128)S(1)} %copy-done.12), channel_id=11, replica_groups=mesh['blk'=8,'ctx_0'=8,'ctx_1'=2,'ctx_2'=2] {'ctx_0','ctx_1','ctx_2'}, dimensions={1}, use_global_device_ids=true | all-gather | bytes 16896 | tf_op jit(solution)/shard_map/all_gather | solution.py:225
  446.5 33.9 %all-gather.25.cloned.1.call-done = bf16[4096,1024]{1,0:T(8,128)(2,1)} async-done(((bf16[128,1024]{1,0:T(8,128)(2,1)}), bf16[4096,1024]{1,0:T(8,128)(2,1)}) %all-gather.25.cloned.1.call-update) | async-done | bytes 8388624 | tf_op jit(solution)/shard_map/all_gather | solution.py:100
  480.3 5.8 %fusion.182 = (bf16[4096,512]{1,0:T(8,128)(2,1)}, bf16[4096,512]{1,0:T(8,128)(2,1)}) fusion(bf16[4096,1024]{1,0:T(8,128)(2,1)} %all-gather.25.cloned.1.call-done), kind=kLoop, calls=%fused_computation.239 | loop fusion | bytes 16777216 | tf_op jit(solution)/shard_map/split | solution.py:100
  486.1 7.0 %reshape.498 = bf16[4096,4,128]{2,1,0:T(4,128)(2,1)} reshape(bf16[4096,512]{1,0:T(8,128)(2,1)} %get-tuple-element.166) | data formatting | bytes 8388608 | tf_op jit(solution)/shard_map/reshape | solution.py:233
  493.1 9.8 %fusion.33 = (f32[4,2,128]{2,1,0:T(2,128)S(1)}, f32[4,4096,128,2]{2,1,3,0:T(8,128)}) fusion(pred[128,4096]{0,1:T(8,128)(4,1)S(1)} %fusion.56, bf16[128,4,2,128]{3,2,1,0:T(2,128)(2,1)S(1)} %reshape.499, bf16[4096,4,128,1]{2,1,0,3:T(4,128)(2,1)} %bitcast.311), kind=kOutput, calls=%fused_computation.50 | convolution fusion | flops 1086323712 | bytes 21762048 | tf_op jit(solution)/shard_map/tkgd,skd->kgts/dot_general | solution.py:230
  502.9 6.5 %copy.149 = bf16[4096,512]{0,1:T(8,128)(2,1)} copy(bf16[4096,512]{1,0:T(8,128)(2,1)} %get-tuple-element.167) | data formatting | bytes 8388608 | tf_op jit(solution)/shard_map/reshape | solution.py:248
  509.3 8.2 %fusion.34 = f32[4,2,128]{2,1,0:T(2,128)S(1)} fusion(f32[4,4096,128,2]{2,1,3,0:T(8,128)} %get-tuple-element.226, f32[4,2,128]{2,1,0:T(2,128)S(1)} %broadcast_maximum_fusion, pred[128,4096]{0,1:T(8,128)(4,1)S(1)} %fusion.56), kind=kLoop, calls=%fused_computation.51 | loop fusion | flops 20970496 | bytes 17309696 | tf_op jit(solution)/shard_map/reduce_sum | solution.py:244
  520.1 6.5 %fusion.110 = bf16[128,4,2,128]{0,3,2,1:T(8,128)(2,1)S(1)} fusion(bf16[4096,4,128,1]{0,2,3,1:T(8,128)(2,1)} %bitcast.310, f32[4,4096,128,2]{2,1,3,0:T(8,128)S(1)} %copy-done, f32[4,2,128]{2,1,0:T(2,128)S(1)} %broadcast_maximum_fusion, pred[128,4096]{0,1:T(8,128)(4,1)S(1)} %fusion.56, f32[128,4,2]{0,2,1:T(2,128)S(1)} %bitcast.326), kind=kOutput, calls=%fused_computation.116 | convolution fusion | flops 1094975488 | bytes 21766144 | tf_op jit(solution)/shard_map/kgts,skd->kgtd/dot_general | solution.py:245
  526.6 19.5 %all-gather.35.cloned.1.call-done = bf16[1,1024,1024]{2,1,0:T(8,128)(2,1)} async-done(((bf16[1,32,1024]{2,1,0:T(8,128)(2,1)}), bf16[1,1024,1024]{2,1,0:T(8,128)(2,1)}) %all-gather.35.cloned.1.call-update) | async-done | bytes 2097168 | tf_op jit(solution)/shard_map/all_gather | solution.py:261
  (207 shorter events, 97.7 us)
Async XLA Ops:
  6.5 78.3 %all-gather.27.cloned.1.call-start = ((), (), s32[]{:S(2)}) async-start(), calls=%async_computation.1 | async-start | bytes 4325376 | tf_op jit(solution)/shard_map/all_gather | solution.py:168
  6.5 8.6 %collective-permute-start.4 = (bf16[1,1024,64]{1,2,0:T(8,128)(2,1)}, bf16[1,1024,64]{1,2,0:T(8,128)(2,1)S(1)}, u32[]{:S(2)}, u32[]{:S(2)}) collective-permute-start(bf16[1,1024,64]{1,2,0:T(8,128)(2,1)} %param.17), channel_id=1, source_target_pairs={{0,32},{32,64},{64,96},{96,128},{128,160},{160,192},{192,224},{224... | collective-permute-start | bytes 393224 | tf_op jit(solution)/shard_map/ppermute | solution.py:106
  15.8 177.7 %all-gather.37.cloned.1.call-start = ((), (), s32[]{:S(2)}) async-start(), calls=%async_computation.6 | async-start | bytes 1671168 | tf_op jit(solution)/shard_map/all_gather | solution.py:34
  15.8 14.6 %collective-permute-start = (bf16[1,2,1024]{2,1,0:T(2,128)(2,1)}, bf16[1,2,1024]{2,1,0:T(2,128)(2,1)S(1)}, u32[]{:S(2)}, u32[]{:S(2)}) collective-permute-start(bf16[1,2,1024]{2,1,0:T(2,128)(2,1)} %param.16), channel_id=1, source_target_pairs={{0,32},{32,64},{64,96},{96,128},{128,160},{160,192},{192,224},{224... | collective-permute-start | bytes 12296 | tf_op jit(solution)/shard_map/ppermute | solution.py:106
  17.0 13.4 %collective-permute-start.3 = (bf16[1,32]{1,0:T(2,128)(2,1)}, bf16[1,32]{1,0:T(2,128)(2,1)S(1)}, u32[]{:S(2)}, u32[]{:S(2)}) collective-permute-start(bf16[1,32]{1,0:T(2,128)(2,1)} %param.19), channel_id=1, source_target_pairs={{0,32},{32,64},{64,96},{96,128},{128,160},{160,192},{192,224},{224... | collective-permute-start | bytes 200 | tf_op jit(solution)/shard_map/ppermute | solution.py:106
  19.1 11.3 %collective-permute-start.2 = (bf16[1,32]{1,0:T(2,128)(2,1)}, bf16[1,32]{1,0:T(2,128)(2,1)S(1)}, u32[]{:S(2)}, u32[]{:S(2)}) collective-permute-start(bf16[1,32]{1,0:T(2,128)(2,1)} %param.20), channel_id=1, source_target_pairs={{0,32},{32,64},{64,96},{96,128},{128,160},{160,192},{192,224},{224... | collective-permute-start | bytes 200 | tf_op jit(solution)/shard_map/ppermute | solution.py:106
  21.0 11.2 %collective-permute-start.1 = (bf16[1,1024,160]{1,2,0:T(8,128)(2,1)}, bf16[1,1024,160]{1,2,0:T(8,128)(2,1)S(1)}, u32[]{:S(2)}, u32[]{:S(2)}) collective-permute-start(bf16[1,1024,160]{1,2,0:T(8,128)(2,1)} %param.18), channel_id=1, source_target_pairs={{0,32},{32,64},{64,96},{96,128},{128,160},{160,192},{192,224},{224... | collective-permute-start | bytes 983048 | tf_op jit(solution)/shard_map/ppermute | solution.py:106
  167.7 57.1 %copy-start.18 = (u32[256]{0:T(256)S(1)}, u32[256]{0:T(256)}, u32[]{:S(2)}) copy-start(u32[256]{0:T(256)} %constant.109) | copy-start | bytes 3076
  167.7 67.1 %copy-start.17 = (u32[256]{0:T(256)S(1)}, u32[256]{0:T(256)}, u32[]{:S(2)}) copy-start(u32[256]{0:T(256)} %constant.114) | copy-start | bytes 3076
  169.4 54.1 %all-gather.29.cloned.1.call-start = ((), (), s32[]{:S(2)}) async-start(), calls=%async_computation.2 | async-start | bytes 2359296 | tf_op jit(solution)/shard_map/all_gather | solution.py:83
  169.4 8.7 %collective-permute-start.7 = (bf16[1,64,1024]{2,1,0:T(8,128)(2,1)}, bf16[1,64,1024]{2,1,0:T(8,128)(2,1)S(1)}, u32[]{:S(2)}, u32[]{:S(2)}) collective-permute-start(bf16[1,64,1024]{2,1,0:T(8,128)(2,1)} %param.23), channel_id=1, source_target_pairs={{0,32},{32,64},{64,96},{96,128},{128,160},{160,192},{192,224},{224... | collective-permute-start | bytes 393224 | tf_op jit(solution)/shard_map/ppermute | solution.py:106
  182.7 77.8 %all-gather.39.cloned.1.call-start = ((), (), s32[]{:S(2)}) async-start(), calls=%async_computation.7 | async-start | bytes 1671168 | tf_op jit(solution)/shard_map/all_gather | solution.py:34
  194.9 69.2 %copy-start.13 = (bf16[1,1024,64]{1,2,0:T(8,128)(2,1)S(1)}, bf16[1,1024,64]{1,2,0:T(8,128)(2,1)}, u32[]{:S(2)}) copy-start(bf16[1,1024,64]{1,2,0:T(8,128)(2,1)} %param.24) | copy-start | bytes 393220
  196.2 76.3 %copy-start.15 = (bf16[1,2048]{1,0:T(2,128)(2,1)S(1)}, bf16[1,2048]{1,0:T(2,128)(2,1)}, u32[]{:S(2)}) copy-start(bf16[1,2048]{1,0:T(2,128)(2,1)} %param.22) | copy-start | bytes 12292
  196.2 77.0 %copy-start.16 = (bf16[1,32]{1,0:T(2,128)(2,1)S(1)}, bf16[1,32]{1,0:T(2,128)(2,1)}, u32[]{:S(2)}) copy-start(bf16[1,32]{1,0:T(2,128)(2,1)} %param.21) | copy-start | bytes 196
  196.2 87.8 %copy-start.12 = (s32[1,128]{1,0:T(1,128)S(1)}, s32[1,128]{1,0:T(1,128)}, u32[]{:S(2)}) copy-start(s32[1,128]{1,0:T(1,128)} %param.15) | copy-start | bytes 1540
  197.1 87.2 %all-gather.31.cloned.1.call-start = ((), (), s32[]{:S(2)}) async-start(), calls=%async_computation.3 | async-start | bytes 6291456 | tf_op jit(solution)/shard_map/all_gather | solution.py:83
  223.5 113.2 %all-gather.41.cloned.1.call-start = ((), (), s32[]{:S(2)}) async-start(), calls=%async_computation.8 | async-start | bytes 5013504 | tf_op jit(solution)/shard_map/all_gather | solution.py:34
  264.0 140.2 %all-gather.33.cloned.1.call-start = ((), (), s32[]{:S(2)}) async-start(), calls=%async_computation.4 | async-start | bytes 4325376 | tf_op jit(solution)/shard_map/all_gather | solution.py:214
  264.1 7.7 %collective-permute-start.8 = (bf16[1,1024,64]{1,2,0:T(8,128)(2,1)S(1)}, bf16[1,1024,64]{1,2,0:T(8,128)(2,1)S(1)}, u32[]{:S(2)}, u32[]{:S(2)}) collective-permute-start(bf16[1,1024,64]{1,2,0:T(8,128)(2,1)S(1)} %copy-done.13), channel_id=1, source_target_pairs={{0,32},{32,64},{64,96},{96,128},{128,160},{160,192},{192,224},{224... | collective-permute-start | bytes 393224 | tf_op jit(solution)/shard_map/ppermute | solution.py:106
  272.4 207.9 %all-gather.25.cloned.1.call-start = ((), (), s32[]{:S(2)}) async-start(), calls=%async_computation | async-start | bytes 8650752 | tf_op jit(solution)/shard_map/all_gather | solution.py:100
  272.5 11.6 %collective-permute-start.6 = (bf16[1,2048]{1,0:T(2,128)(2,1)S(1)}, bf16[1,2048]{1,0:T(2,128)(2,1)S(1)}, u32[]{:S(2)}, u32[]{:S(2)}) collective-permute-start(bf16[1,2048]{1,0:T(2,128)(2,1)S(1)} %copy-done.15), channel_id=1, source_target_pairs={{0,32},{32,64},{64,96},{96,128},{128,160},{160,192},{192,224},{224... | collective-permute-start | bytes 12296 | tf_op jit(solution)/shard_map/ppermute | solution.py:106
  273.1 10.9 %collective-permute-start.5 = (bf16[1,32]{1,0:T(2,128)(2,1)S(1)}, bf16[1,32]{1,0:T(2,128)(2,1)S(1)}, u32[]{:S(2)}, u32[]{:S(2)}) collective-permute-start(bf16[1,32]{1,0:T(2,128)(2,1)S(1)} %copy-done.16), channel_id=1, source_target_pairs={{0,32},{32,64},{64,96},{96,128},{128,160},{160,192},{192,224},{224... | collective-permute-start | bytes 200 | tf_op jit(solution)/shard_map/ppermute | solution.py:106
  345.4 11.0 %slice-start = ((f32[8,2049,64]{1,2,0:T(8,128)}), f32[8,1,64]{1,2,0:T(8,128)S(1)}, s32[]{:S(2)}) async-start(f32[8,2049,64]{1,2,0:T(8,128)} %all-gather.41.cloned.1.call-done), calls=%async_computation.9 | async-start | bytes 524288 | tf_op jit(solution)/shard_map/slice | solution.py:36
  345.4 11.1 %copy-start.5 = (f32[128,32,64]{0,2,1:T(8,128)S(1)}, f32[128,32,64]{0,2,1:T(8,128)}, u32[]{:S(2)}) copy-start(f32[128,32,64]{0,2,1:T(8,128)} %reshape.485) | copy-start | bytes 3145732
  356.5 7.1 %copy-start.1 = (bf16[8,2,2,64,1024]{4,3,2,1,0:T(8,128)(2,1)S(1)}, bf16[8,2,2,64,1024]{4,3,2,1,0:T(8,128)(2,1)}, u32[]{:S(2)}) copy-start(bf16[8,2,2,64,1024]{4,3,2,1,0:T(8,128)(2,1)} %copy.121) | copy-start | bytes 12582916
  356.5 7.1 %copy-start.6 = (bf16[1,128,1024]{2,1,0:T(8,128)(2,1)S(1)}, bf16[1,128,1024]{2,1,0:T(8,128)(2,1)}, u32[]{:S(2)}) copy-start(bf16[1,128,1024]{2,1,0:T(8,128)(2,1)} %param.14) | copy-start | bytes 786436
  363.1 41.1 %copy-start.11 = (f32[1,1,1024]{2,1,0:T(1,128)S(1)}, f32[1,1,1024]{2,1,0:T(1,128)}, u32[]{:S(2)}) copy-start(f32[1,1,1024]{2,1,0:T(1,128)} %get-tuple-element.184) | copy-start | bytes 12292
  364.4 44.3 %copy-start.14 = (bf16[1,32,1024]{2,1,0:T(8,128)(2,1)S(1)}, bf16[1,32,1024]{2,1,0:T(8,128)(2,1)}, u32[]{:S(2)}) copy-start(bf16[1,32,1024]{2,1,0:T(8,128)(2,1)} %param.25) | copy-start | bytes 196612
  408.7 137.4 %all-gather.35.cloned.1.call-start = ((), (), s32[]{:S(2)}) async-start(), calls=%async_computation.5 | async-start | bytes 2162688 | tf_op jit(solution)/shard_map/all_gather | solution.py:261
  408.8 36.9 %collective-permute-start.9 = (bf16[1,32,1024]{2,1,0:T(8,128)(2,1)S(1)}, bf16[1,32,1024]{2,1,0:T(8,128)(2,1)S(1)}, u32[]{:S(2)}, u32[]{:S(2)}) collective-permute-start(bf16[1,32,1024]{2,1,0:T(8,128)(2,1)S(1)} %copy-done.14), channel_id=1, source_target_pairs={{0,32},{32,64},{64,96},{96,128},{128,160},{160,192},{192,224},{224... | collective-permute-start | bytes 196616 | tf_op jit(solution)/shard_map/ppermute | solution.py:106
  509.3 10.8 %copy-start = (f32[4,4096,128,2]{2,1,3,0:T(8,128)S(1)}, f32[4,4096,128,2]{2,1,3,0:T(8,128)}, u32[]{:S(2)}) copy-start(f32[4,4096,128,2]{2,1,3,0:T(8,128)} %get-tuple-element.226) | copy-start | bytes 50331652
  (7 other events, 14.2 us)
Sparse Core Ops, SparseCore 0:
  15.9 68.8 all-gather.26
  169.5 14.8 all-gather.36
  186.2 37.2 all-gather.28
  225.1 29.6 all-gather.38
  256.5 20.8 all-gather.30
  279.0 57.6 all-gather.40
  338.5 65.6 all-gather.32
  408.8 71.4 all-gather.24
  482.2 63.8 all-gather.34
where the time goes:
time: 564 us; the launch traced here: 556 us
  waiting for transfers between devices  223 us (40%)
  local copies, waits for them, and re-layouts  130 us (23%)
  blocking collectives  52.9 us (9%)
  between operations  49.7 us (9%)
  matrix products  49.1 us (9%)
  other arithmetic  24.8 us (4%)
  starting transfers between devices  22.4 us (4%)
    dynamic_update_slice x2, local copies, waits for them, and re-layouts, layer_pair(): (local_state, ignored), mixed = lax.scan(span_update, start_carry, blocks)  50.9 us
    all_gather x1, waiting for transfers between devices, layer_pair(): lax.all_gather(w_mamba_in, CTX, axis=1, tiled=True)  50 us
    all_gather x1, waiting for transfers between devices, layer_pair(): lax.all_gather(w_qkv, CTX, axis=1, tiled=True)  39.8 us
    all_gather x3, waiting for transfers between devices, gathered_once(): both, at, found = (lax.all_gather(jnp.concatenate(lines), axis), 0, {})  37.1 us
    all_gather x1, waiting for transfers between devices, in_one_piece(): lax.all_gather(both, axis, axis=dim, tiled=True)  33.9 us
    all_gather x1, blocking collectives, layer_pair(): lax.all_gather(segment, CTX, axis=0, tiled=True)  32.5 us
    all_gather x2, waiting for transfers between devices, all_blocks(): blocks = lax.all_gather(blocks, axes[k])  26.3 us
    ppermute x10, starting transfers between devices, from_behind(): return lax.ppermute(value, axis, pairs)  22.1 us
  transfers between devices with their start and end apart: 19, of which 10 were waited for; matrix products, arithmetic and copies ran while one was open for 20% of the time, Pallas kernels for 0%

commit v1 on v0

--- a/solution.py
+++ b/solution.py
@@ -211,7 +211,9 @@
     )
     hidden = rms_norm(first, norm_gain[1]).astype(jnp.bfloat16)
     projected = jnp.dot(
-        hidden, lax.all_gather(w_qkv, CTX, axis=1, tiled=True), preferred_element_type=jnp.float32
+        hidden,
+        jnp.concatenate(lax.all_to_all(jnp.stack([w_qkv] * lax.axis_size(CTX)), CTX, 0, 0), axis=1),
+        preferred_element_type=jnp.float32,
     ).astype(jnp.bfloat16)
     groups = QUERY_HEADS // KV_HEADS
     query = projected[:, : QUERY_HEADS * ATTN_DIM].reshape(rows, KV_HEADS, groups, ATTN_DIM)

time: 564 us -> 611 us (1.083)
  waiting for transfers between devices: 223 us -> 252 us
  starting transfers between devices: 22.4 us -> 39.5 us
    all_gather x3, waiting for transfers between devices: 37.1 us -> 103 us  [gathered_once(): both, at, found = (lax.all_gather(jnp.concatenate(lines), axis), 0, {})]
    all_gather x1 -> x0, waiting for transfers between devices: 39.8 us -> none  [layer_pair(): lax.all_gather(w_qkv, CTX, axis=1, tiled=True)]
    all_to_all x0 -> x1, starting transfers between devices: none -> 16.1 us  [layer_pair(): lax.all_to_all(jnp.stack([w_qkv] * lax.axis_size(CTX)), CTX, 0, 0)]
  transfers between devices with their start and end apart: 19 -> 19, of which waited for: 10 -> 9; matrix products, arithmetic and copies ran while one was open for 20% -> 19% of each run, Pallas kernels for 0% -> 0%
where the time goes in v1:
time: 611 us; the launch traced here: 603 us
  waiting for transfers between devices  252 us (41%)
  local copies, waits for them, and re-layouts  132 us (22%)
  blocking collectives  52.2 us (9%)
  between operations  50.1 us (8%)
  matrix products  49.1 us (8%)
  starting transfers between devices  39.5 us (6%)
  other arithmetic  24.8 us (4%)
    all_gather x3, waiting for transfers between devices, gathered_once(): both, at, found = (lax.all_gather(jnp.concatenate(lines), axis), 0, {})  103 us
    dynamic_update_slice x2, local copies, waits for them, and re-layouts, layer_pair(): (local_state, ignored), mixed = lax.scan(span_update, start_carry, blocks)  50.9 us
    all_gather x1, waiting for transfers between devices, layer_pair(): lax.all_gather(w_mamba_in, CTX, axis=1, tiled=True)  49.9 us
    all_gather x1, waiting for transfers between devices, in_one_piece(): lax.all_gather(both, axis, axis=dim, tiled=True)  36.6 us
    all_gather x1, blocking collectives, layer_pair(): lax.all_gather(segment, CTX, axis=0, tiled=True)  31.9 us
    all_gather x2, waiting for transfers between devices, all_blocks(): blocks = lax.all_gather(blocks, axes[k])  26.4 us
    ppermute x10, starting transfers between devices, from_behind(): return lax.ppermute(value, axis, pairs)  23.1 us
    squeeze x12, local copies, waits for them, and re-layouts, entering_2(): so_far = combine(so_far, jax.tree.map(lambda part: part[k], pieces))  21.3 us
  transfers between devices with their start and end apart: 19, of which 9 were waited for; matrix products, arithmetic and copies ran while one was open for 19% of the time, Pallas kernels for 0%

profile of v1, /device:TPU:1, one launch (start us, length us, event | category | flops | bytes accessed | tf_op | source)
XLA Modules:
  0.0 602.5 jit_solution(11947317060796020577)
XLA Ops:
  6.5 3.6 collective-permute-start.4
  10.1 5.0 collective-permute-done.4
  34.9 49.9 %all-gather.25.cloned.1.call-done = bf16[1,1024,2048]{1,2,0:T(8,128)(2,1)} async-done(((bf16[1,1024,64]{1,2,0:T(8,128)(2,1)}), bf16[1,1024,2048]{1,2,0:T(8,128)(2,1)}) %all-gather.25.cloned.1.call-update) | async-done | bytes 4194320 | tf_op jit(solution)/shard_map/all_gather | solution.py:168
  84.8 3.8 fusion.46
  90.8 76.3 %while.15 = (s32[]{:T(128)}, f32[32,64,64]{2,1,0:T(8,128)S(1)}, s32[]{:T(128)}, f32[2,64,32,64]{1,0,3,2:T(2,128)}, s32[2,64]{1,0:T(2,128)}, /*index=5*/f32[2,64,...) while((s32[]{:T(128)}, f32[32,64,64]{2,1,0:T(8,128)S(1)}, ...), condition=%wide.region_3.4_spmd.clone, body=%wide.region_1.3_spmd.clone.sunk | while | flops 306858144 | bytes 9277010 | solution.py:184
  95.3 3.0 convolution_bitcast_fusion.2
  102.9 25.5 %dynamic_update_slice.6 = f32[2,64,32,64]{1,0,3,2:T(2,128)} dynamic-update-slice(f32[2,64,32,64]{1,0,3,2:T(2,128)} %get-tuple-element.314, f32[1,64,32,64]{1,0,3,2:T(1,128)S(1)} %bitcast.295, s32[]{:T(128)S(6)} %copy.186, s32[]{:T(128)} %constant.29.clone.1..sunk, s32[]{:T(128)} %constant.29.clone.1..sunk, s32[]{:T(128)} %constant.29.clone.1..sunk) | dynamic-update-slice | bytes 1048580 | tf_op jit(solution)/shard_map/while/body/jit(dynamic_update_index_in_dim)/dynamic_update_slice | solution.py:184
  141.1 25.5 %dynamic_update_slice.6 = f32[2,64,32,64]{1,0,3,2:T(2,128)} dynamic-update-slice(f32[2,64,32,64]{1,0,3,2:T(2,128)} %get-tuple-element.314, f32[1,64,32,64]{1,0,3,2:T(1,128)S(1)} %bitcast.295, s32[]{:T(128)S(6)} %copy.186, s32[]{:T(128)} %constant.29.clone.1..sunk, s32[]{:T(128)} %constant.29.clone.1..sunk, s32[]{:T(128)} %constant.29.clone.1..sunk) | dynamic-update-slice | bytes 1048580 | tf_op jit(solution)/shard_map/while/body/jit(dynamic_update_index_in_dim)/dynamic_update_slice | solution.py:184
  171.9 6.0 collective-permute-done.7
  177.9 4.6 all_gather.76
  186.2 3.8 all-reduce.3
  196.9 26.4 %all-gather.27.cloned.1.call-done = bf16[16,64,1024]{2,1,0:T(8,128)(2,1)} async-done(((bf16[2,64,1024]{2,1,0:T(8,128)(2,1)}), bf16[16,64,1024]{2,1,0:T(8,128)(2,1)}) %all-gather.27.cloned.1.call-update) | async-done | bytes 2097168 | tf_op jit(solution)/shard_map/all_gather | solution.py:83
  228.2 3.1 all-reduce.4
  239.5 8.9 %all-reduce.5 = s32[16]{0:T(128)S(1)} all-reduce(s32[16]{0:T(128)S(1)} %fusion.169), channel_id=5, replica_groups=mesh['blk'=8,'ctx_0'=8,'ctx_1'=2,'ctx_2'=2] {'ctx_0'}, use_global_device_ids=true, to_apply=%add.5 | all-reduce | flops 16 | bytes 128
  267.0 4.7 collective-permute-done.8
  274.4 16.1 %all-to-all-start = ((bf16[32,1024,64]{1,2,0:T(8,128)(2,1)}), bf16[32,1024,64]{1,2,0:T(8,128)(2,1)}, u32[]{:S(2)}, u32[]{:S(2)}) async-start(bf16[32,1024,64]{1,2,0:T(8,128)(2,1)} %stack.3), calls=%async_computation | async-start | bytes 8388608 | tf_op jit(solution)/shard_map/all_to_all | solution.py:215
  302.2 5.0 copy.122
  307.5 3.4 reshape.492
  317.6 102.7 %all-gather.37.cloned.1.call-done = f32[8,2049,64]{1,2,0:T(8,128)} async-done(((f32[1,2049,64]{1,2,0:T(8,128)}), f32[8,2049,64]{1,2,0:T(8,128)}) %all-gather.37.cloned.1.call-update) | async-done | bytes 4196368 | tf_op jit(solution)/shard_map/all_gather | solution.py:34
  420.3 3.7 fusion.178
  440.1 6.5 %multiply_reduce_fusion = (f32[128]{0:T(128)S(1)}, f32[128,32,64]{0,2,1:T(8,128)S(1)}) fusion(f32[32]{0:T(128)S(1)} %bitcast_convert_fusion, f32[128,2048]{0,1:T(8,128)S(1)} %copy.121, f32[128,32,64]{0,2,1:T(8,128)S(1)} %copy-done.5, f32[128,32]{0,1:T(8,128)S(1)} %exponential_select_fusion.2, f32[32,64,64]{2,1,0:T(8,128)} %bitcast.297, ...), kind=kOutput, calls=%fused_computation.74 | convolution fusion | flops 207748992 | bytes 15780236 | tf_op jit(solution)/shard_map/tn,hpn->thp/dot_general | solution.py:199
  447.9 3.7 convolution_convert_fusion
  452.5 3.4 collective-permute-start.9
  455.9 31.9 %all-gather.9 = s32[1,4096]{1,0:T(1,128)S(1)} all-gather(s32[1,128]{1,0:T(1,128)S(1)} %copy-done.11), channel_id=11, replica_groups=mesh['blk'=8,'ctx_0'=8,'ctx_1'=2,'ctx_2'=2] {'ctx_0','ctx_1','ctx_2'}, dimensions={1}, use_global_device_ids=true | all-gather | bytes 16896 | tf_op jit(solution)/shard_map/all_gather | solution.py:227
  490.5 36.6 %all-gather.23.cloned.1.call-done = bf16[4096,1024]{1,0:T(8,128)(2,1)} async-done(((bf16[128,1024]{1,0:T(8,128)(2,1)}), bf16[4096,1024]{1,0:T(8,128)(2,1)}) %all-gather.23.cloned.1.call-update) | async-done | bytes 8388624 | tf_op jit(solution)/shard_map/all_gather | solution.py:100
  527.1 5.8 fusion.177
  532.9 7.0 %reshape.507 = bf16[4096,4,128]{2,1,0:T(4,128)(2,1)} reshape(bf16[4096,512]{1,0:T(8,128)(2,1)} %get-tuple-element.166) | data formatting | bytes 8388608 | tf_op jit(solution)/shard_map/reshape | solution.py:235
  539.9 9.8 %fusion.33 = (f32[4,2,128]{2,1,0:T(2,128)S(1)}, f32[4,4096,128,2]{2,1,3,0:T(8,128)}) fusion(pred[128,4096]{0,1:T(8,128)(4,1)S(1)} %fusion.51, bf16[128,4,2,128]{3,2,1,0:T(2,128)(2,1)S(1)} %reshape.508, bf16[4096,4,128,1]{2,1,0,3:T(4,128)(2,1)} %bitcast.311), kind=kOutput, calls=%fused_computation.50 | convolution fusion | flops 1086323712 | bytes 21762048 | tf_op jit(solution)/shard_map/tkgd,skd->kgts/dot_general | solution.py:232
  549.6 6.5 %copy.150 = bf16[4096,512]{0,1:T(8,128)(2,1)} copy(bf16[4096,512]{1,0:T(8,128)(2,1)} %get-tuple-element.167) | data formatting | bytes 8388608 | tf_op jit(solution)/shard_map/reshape | solution.py:250
  556.1 8.2 %fusion.34 = f32[4,2,128]{2,1,0:T(2,128)S(1)} fusion(f32[4,4096,128,2]{2,1,3,0:T(8,128)} %get-tuple-element.226, f32[4,2,128]{2,1,0:T(2,128)S(1)} %broadcast_maximum_fusion, pred[128,4096]{0,1:T(8,128)(4,1)S(1)} %fusion.51), kind=kLoop, calls=%fused_computation.51 | loop fusion | flops 20970496 | bytes 17309696 | tf_op jit(solution)/shard_map/reduce_sum | solution.py:246
  566.9 6.5 %fusion.105 = bf16[128,4,2,128]{0,3,2,1:T(8,128)(2,1)S(1)} fusion(bf16[4096,4,128,1]{0,2,3,1:T(8,128)(2,1)} %bitcast.310, f32[4,4096,128,2]{2,1,3,0:T(8,128)S(1)} %copy-done, f32[4,2,128]{2,1,0:T(2,128)S(1)} %broadcast_maximum_fusion, pred[128,4096]{0,1:T(8,128)(4,1)S(1)} %fusion.51, f32[128,4,2]{0,2,1:T(2,128)S(1)} %bitcast.327), kind=kOutput, calls=%fused_computation.114 | convolution fusion | flops 1094975488 | bytes 21766144 | tf_op jit(solution)/shard_map/kgts,skd->kgtd/dot_general | solution.py:247
  573.4 19.3 %all-gather.31.cloned.1.call-done = bf16[1,1024,1024]{2,1,0:T(8,128)(2,1)} async-done(((bf16[1,32,1024]{2,1,0:T(8,128)(2,1)}), bf16[1,1024,1024]{2,1,0:T(8,128)(2,1)}) %all-gather.31.cloned.1.call-update) | async-done | bytes 2097168 | tf_op jit(solution)/shard_map/all_gather | solution.py:263
  (205 shorter events, 100.2 us)
Async XLA Ops:
  6.5 78.3 %all-gather.25.cloned.1.call-start = ((), (), s32[]{:S(2)}) async-start(), calls=%async_computation.2 | async-start | bytes 4325376 | tf_op jit(solution)/shard_map/all_gather | solution.py:168
  6.5 8.6 %collective-permute-start.4 = (bf16[1,1024,64]{1,2,0:T(8,128)(2,1)}, bf16[1,1024,64]{1,2,0:T(8,128)(2,1)S(1)}, u32[]{:S(2)}, u32[]{:S(2)}) collective-permute-start(bf16[1,1024,64]{1,2,0:T(8,128)(2,1)} %param.17), channel_id=1, source_target_pairs={{0,32},{32,64},{64,96},{96,128},{128,160},{160,192},{192,224},{224... | collective-permute-start | bytes 393224 | tf_op jit(solution)/shard_map/ppermute | solution.py:106
  15.8 177.5 %all-gather.33.cloned.1.call-start = ((), (), s32[]{:S(2)}) async-start(), calls=%async_computation.6 | async-start | bytes 1671168 | tf_op jit(solution)/shard_map/all_gather | solution.py:34
  15.8 14.7 %collective-permute-start = (bf16[1,2,1024]{2,1,0:T(2,128)(2,1)}, bf16[1,2,1024]{2,1,0:T(2,128)(2,1)S(1)}, u32[]{:S(2)}, u32[]{:S(2)}) collective-permute-start(bf16[1,2,1024]{2,1,0:T(2,128)(2,1)} %param.16), channel_id=1, source_target_pairs={{0,32},{32,64},{64,96},{96,128},{128,160},{160,192},{192,224},{224... | collective-permute-start | bytes 12296 | tf_op jit(solution)/shard_map/ppermute | solution.py:106
  17.0 13.5 %collective-permute-start.3 = (bf16[1,32]{1,0:T(2,128)(2,1)}, bf16[1,32]{1,0:T(2,128)(2,1)S(1)}, u32[]{:S(2)}, u32[]{:S(2)}) collective-permute-start(bf16[1,32]{1,0:T(2,128)(2,1)} %param.19), channel_id=1, source_target_pairs={{0,32},{32,64},{64,96},{96,128},{128,160},{160,192},{192,224},{224... | collective-permute-start | bytes 200 | tf_op jit(solution)/shard_map/ppermute | solution.py:106
  19.1 11.4 %collective-permute-start.2 = (bf16[1,32]{1,0:T(2,128)(2,1)}, bf16[1,32]{1,0:T(2,128)(2,1)S(1)}, u32[]{:S(2)}, u32[]{:S(2)}) collective-permute-start(bf16[1,32]{1,0:T(2,128)(2,1)} %param.20), channel_id=1, source_target_pairs={{0,32},{32,64},{64,96},{96,128},{128,160},{160,192},{192,224},{224... | collective-permute-start | bytes 200 | tf_op jit(solution)/shard_map/ppermute | solution.py:106
  21.0 11.2 %collective-permute-start.1 = (bf16[1,1024,160]{1,2,0:T(8,128)(2,1)}, bf16[1,1024,160]{1,2,0:T(8,128)(2,1)S(1)}, u32[]{:S(2)}, u32[]{:S(2)}) collective-permute-start(bf16[1,1024,160]{1,2,0:T(8,128)(2,1)} %param.18), channel_id=1, source_target_pairs={{0,32},{32,64},{64,96},{96,128},{128,160},{160,192},{192,224},{224... | collective-permute-start | bytes 983048 | tf_op jit(solution)/shard_map/ppermute | solution.py:106
  167.5 57.3 %copy-start.17 = (u32[256]{0:T(256)S(1)}, u32[256]{0:T(256)}, u32[]{:S(2)}) copy-start(u32[256]{0:T(256)} %constant.109) | copy-start | bytes 3076
  167.5 67.2 %copy-start.16 = (u32[256]{0:T(256)S(1)}, u32[256]{0:T(256)}, u32[]{:S(2)}) copy-start(u32[256]{0:T(256)} %constant.114) | copy-start | bytes 3076
  169.2 54.1 %all-gather.27.cloned.1.call-start = ((), (), s32[]{:S(2)}) async-start(), calls=%async_computation.3 | async-start | bytes 2359296 | tf_op jit(solution)/shard_map/all_gather | solution.py:83
  169.3 8.7 %collective-permute-start.7 = (bf16[1,64,1024]{2,1,0:T(8,128)(2,1)}, bf16[1,64,1024]{2,1,0:T(8,128)(2,1)S(1)}, u32[]{:S(2)}, u32[]{:S(2)}) collective-permute-start(bf16[1,64,1024]{2,1,0:T(8,128)(2,1)} %param.23), channel_id=1, source_target_pairs={{0,32},{32,64},{64,96},{96,128},{128,160},{160,192},{192,224},{224... | collective-permute-start | bytes 393224 | tf_op jit(solution)/shard_map/ppermute | solution.py:106
  182.5 78.0 %all-gather.35.cloned.1.call-start = ((), (), s32[]{:S(2)}) async-start(), calls=%async_computation.7 | async-start | bytes 1671168 | tf_op jit(solution)/shard_map/all_gather | solution.py:34
  194.7 69.4 %copy-start.12 = (bf16[1,1024,64]{1,2,0:T(8,128)(2,1)S(1)}, bf16[1,1024,64]{1,2,0:T(8,128)(2,1)}, u32[]{:S(2)}) copy-start(bf16[1,1024,64]{1,2,0:T(8,128)(2,1)} %param.24) | copy-start | bytes 393220
  196.9 105.3 %all-gather.29.cloned.1.call-start = ((), (), s32[]{:S(2)}) async-start(), calls=%async_computation.4 | async-start | bytes 6291456 | tf_op jit(solution)/shard_map/all_gather | solution.py:83
  223.3 197.0 %all-gather.37.cloned.1.call-start = ((), (), s32[]{:S(2)}) async-start(), calls=%async_computation.8 | async-start | bytes 5013504 | tf_op jit(solution)/shard_map/all_gather | solution.py:34
  264.1 7.7 %collective-permute-start.8 = (bf16[1,1024,64]{1,2,0:T(8,128)(2,1)S(1)}, bf16[1,1024,64]{1,2,0:T(8,128)(2,1)S(1)}, u32[]{:S(2)}, u32[]{:S(2)}) collective-permute-start(bf16[1,1024,64]{1,2,0:T(8,128)(2,1)S(1)} %copy-done.12), channel_id=1, source_target_pairs={{0,32},{32,64},{64,96},{96,128},{128,160},{160,192},{192,224},{224... | collective-permute-start | bytes 393224 | tf_op jit(solution)/shard_map/ppermute | solution.py:106
  274.4 16.2 %copy-start.14 = (bf16[1,2048]{1,0:T(2,128)(2,1)S(1)}, bf16[1,2048]{1,0:T(2,128)(2,1)}, u32[]{:S(2)}) copy-start(bf16[1,2048]{1,0:T(2,128)(2,1)} %param.22) | copy-start | bytes 12292
  274.4 16.5 %copy-start.15 = (bf16[1,32]{1,0:T(2,128)(2,1)S(1)}, bf16[1,32]{1,0:T(2,128)(2,1)}, u32[]{:S(2)}) copy-start(bf16[1,32]{1,0:T(2,128)(2,1)} %param.21) | copy-start | bytes 196
  274.4 27.5 %copy-start.11 = (s32[1,128]{1,0:T(1,128)S(1)}, s32[1,128]{1,0:T(1,128)}, u32[]{:S(2)}) copy-start(s32[1,128]{1,0:T(1,128)} %param.15) | copy-start | bytes 1540
  274.4 173.5 %all-to-all-start = ((bf16[32,1024,64]{1,2,0:T(8,128)(2,1)}), bf16[32,1024,64]{1,2,0:T(8,128)(2,1)}, u32[]{:S(2)}, u32[]{:S(2)}) async-start(bf16[32,1024,64]{1,2,0:T(8,128)(2,1)} %stack.3), calls=%async_computation | async-start | bytes 8388608 | tf_op jit(solution)/shard_map/all_to_all | solution.py:215
  290.5 236.6 %all-gather.23.cloned.1.call-start = ((), (), s32[]{:S(2)}) async-start(), calls=%async_computation.1 | async-start | bytes 8650752 | tf_op jit(solution)/shard_map/all_gather | solution.py:100
  290.6 11.4 %collective-permute-start.6 = (bf16[1,2048]{1,0:T(2,128)(2,1)S(1)}, bf16[1,2048]{1,0:T(2,128)(2,1)S(1)}, u32[]{:S(2)}, u32[]{:S(2)}) collective-permute-start(bf16[1,2048]{1,0:T(2,128)(2,1)S(1)} %copy-done.14), channel_id=1, source_target_pairs={{0,32},{32,64},{64,96},{96,128},{128,160},{160,192},{192,224},{224... | collective-permute-start | bytes 12296 | tf_op jit(solution)/shard_map/ppermute | solution.py:106
  290.9 11.0 %collective-permute-start.5 = (bf16[1,32]{1,0:T(2,128)(2,1)S(1)}, bf16[1,32]{1,0:T(2,128)(2,1)S(1)}, u32[]{:S(2)}, u32[]{:S(2)}) collective-permute-start(bf16[1,32]{1,0:T(2,128)(2,1)S(1)} %copy-done.15), channel_id=1, source_target_pairs={{0,32},{32,64},{64,96},{96,128},{128,160},{160,192},{192,224},{224... | collective-permute-start | bytes 200 | tf_op jit(solution)/shard_map/ppermute | solution.py:106
  302.2 5.0 copy-start.3
  429.0 10.9 %slice-start = ((f32[8,2049,64]{1,2,0:T(8,128)}), f32[8,1,64]{1,2,0:T(8,128)S(1)}, s32[]{:S(2)}) async-start(f32[8,2049,64]{1,2,0:T(8,128)} %all-gather.37.cloned.1.call-done), calls=%async_computation.9 | async-start | bytes 524288 | tf_op jit(solution)/shard_map/slice | solution.py:36
  429.0 11.0 %copy-start.5 = (f32[128,32,64]{0,2,1:T(8,128)S(1)}, f32[128,32,64]{0,2,1:T(8,128)}, u32[]{:S(2)}) copy-start(f32[128,32,64]{0,2,1:T(8,128)} %reshape.492) | copy-start | bytes 3145732
  440.1 7.0 %copy-start.1 = (bf16[8,2,2,64,1024]{4,3,2,1,0:T(8,128)(2,1)S(1)}, bf16[8,2,2,64,1024]{4,3,2,1,0:T(8,128)(2,1)}, u32[]{:S(2)}) copy-start(bf16[8,2,2,64,1024]{4,3,2,1,0:T(8,128)(2,1)} %copy.122) | copy-start | bytes 12582916
  440.1 7.0 %copy-start.6 = (bf16[1,128,1024]{2,1,0:T(8,128)(2,1)S(1)}, bf16[1,128,1024]{2,1,0:T(8,128)(2,1)}, u32[]{:S(2)}) copy-start(bf16[1,128,1024]{2,1,0:T(8,128)(2,1)} %param.14) | copy-start | bytes 786436
  447.9 4.6 copy-start.13
  452.4 140.3 %all-gather.31.cloned.1.call-start = ((), (), s32[]{:S(2)}) async-start(), calls=%async_computation.5 | async-start | bytes 2162688 | tf_op jit(solution)/shard_map/all_gather | solution.py:263
  452.5 37.2 %collective-permute-start.9 = (bf16[1,32,1024]{2,1,0:T(8,128)(2,1)S(1)}, bf16[1,32,1024]{2,1,0:T(8,128)(2,1)S(1)}, u32[]{:S(2)}, u32[]{:S(2)}) collective-permute-start(bf16[1,32,1024]{2,1,0:T(8,128)(2,1)S(1)} %copy-done.13), channel_id=1, source_target_pairs={{0,32},{32,64},{64,96},{96,128},{128,160},{160,192},{192,224},{224... | collective-permute-start | bytes 196616 | tf_op jit(solution)/shard_map/ppermute | solution.py:106
  556.1 10.8 %copy-start = (f32[4,4096,128,2]{2,1,3,0:T(8,128)S(1)}, f32[4,4096,128,2]{2,1,3,0:T(8,128)}, u32[]{:S(2)}) copy-start(f32[4,4096,128,2]{2,1,3,0:T(8,128)} %get-tuple-element.226) | copy-start | bytes 50331652
  (6 other events, 10.0 us)
Sparse Core Ops, SparseCore 0:
  15.9 68.8 all-gather.24
  169.3 14.8 all-gather.32
  186.0 37.2 all-gather.26
  224.9 29.6 all-gather.34
  256.3 20.9 all-gather.28
  278.9 141.3 all-gather.36
  452.5 74.5 all-gather.22
  529.0 63.6 all-gather.30
